TPU v7x, 32 devices: a whole 2x2x4 slice. The times are simulated.
32 devices in a mesh: seq: 8 (over z, y), tp: 4 (over x, core).
Axes of the slice: x: 2, y: 2, z: 4, core: 2. Of those that a mesh axis runs over, the one named last changes fastest.
Arguments:
- layer_activation: bfloat16 [3072, 2048], P('seq', 'tp'), may hold values from -6 to 6
- sequence_label: int32 [3072], P('seq'), may hold values from 0 to 2, as said below
- sequence_extents: int32 [2], replicated, may hold values from 1 to 1920, as said below
- destination_slots: int32 [2], replicated, may hold values from 0 to 7, as said below
- entry_layernorm_coef: float32 [2048], replicated, may hold values from 0.5 to 1.5
- lagged_blend_coefs: float32 [6, 2048], replicated, may hold values from 0 to 1
- query_matrix: bfloat16 [2048, 2048], P(None, 'tp'), may hold values from -0.125 to 0.125
- lookup_matrix: bfloat16 [2048, 2048], P(None, 'tp'), may hold values from -0.125 to 0.125
- content_matrix: bfloat16 [2048, 2048], P(None, 'tp'), may hold values from -0.125 to 0.125
- readout_matrix: bfloat16 [2048, 2048], P('tp'), may hold values from -0.125 to 0.125
- forgetting_narrow_matrix: bfloat16 [2048, 96], replicated, may hold values from -0.125 to 0.125
- forgetting_widen_matrix: bfloat16 [96, 2048], P(None, 'tp'), may hold values from -2.5 to 2.5
- forgetting_offset: float32 [2048], P('tp'), may hold values from -11 to -3.5
- stepsize_narrow_matrix: bfloat16 [2048, 96], replicated, may hold values from -0.125 to 0.125
- stepsize_widen_matrix: bfloat16 [96, 2048], P(None, 'tp'), may hold values from -0.625 to 0.625
- stepsize_offset: float32 [2048], P('tp'), may hold values from -4 to 4
- gating_narrow_matrix: bfloat16 [2048, 256], replicated, may hold values from -0.125 to 0.125
- gating_widen_matrix: bfloat16 [256, 2048], P(None, 'tp'), may hold values from -0.375 to 0.375
- erasure_lookup_coef: float32 [2048], P('tp'), may hold values from 0.5 to 1.5
- lookup_step_fraction: float32 [2048], P('tp'), may hold values from 0 to 1
- diagonal_reward_coef: float32 [2048], P('tp'), may hold values from -3 to 3
- group_layernorm_coef: float32 [2048], P('tp'), may hold values from 0.5 to 1.5
Outputs:
- mixed: bfloat16 [3072, 2048], P('seq', 'tp')
- final_states: float32 [8, 32, 64, 64], P('seq', 'tp')
- final_rows: bfloat16 [8, 2048], P('seq', 'tp')
Inputs may be any that keep to these rules, and one draw needn't show every extreme that they name: `sequence_label`: token p is in prompt 0 for p < sequence_extents[0], in prompt 1 for the next sequence_extents[1] tokens, and padding (2) after them; at least one padding token. `sequence_extents`: one length is exactly 1920, the other at least 768; their sum is under 3072. `destination_slots`: the two owners differ, and one of them is the last index of seq.
All inputs are finite; a program needn't handle non-finite values.
Results may differ from a plain program's by a relative error of at most 0.012.
Values may be sent and summed in bfloat16 or wider, within the bound.
A program may use at most 128 MiB of HBM per device.

v0:
```python
import jax
import jax.numpy as jnp
from jax import lax
from jax.sharding import PartitionSpec as P

CHANNELS_PER_ONE = 64
PROMPTS = 2
EPS = 1e-05
GROUP_EPS = 0.00064


def from_behind(array, axis, by):
    length = lax.axis_size(axis)
    pairs = [(i, i + by) for i in range(length) if 0 <= i + by < length]
    return lax.ppermute(array, axis, pairs)


def broadcast(value, axis, source):
    kept = jnp.where(lax.axis_index(axis) == source, value, 0).astype(value.dtype)
    return lax.psum(kept, axis)


def matmul(left, right):
    return jnp.dot(left, right, preferred_element_type=jnp.float32)


def compose(earlier_map, later_map):
    return jnp.einsum("hij,hjk->hik", earlier_map, later_map, precision=lax.Precision.HIGHEST)


def on_device(
    layer_activation,
    sequence_label,
    sequence_extents,
    destination_slots,
    entry_layernorm_coef,
    lagged_blend_coefs,
    query_matrix,
    lookup_matrix,
    content_matrix,
    readout_matrix,
    forgetting_narrow_matrix,
    forgetting_widen_matrix,
    forgetting_offset,
    stepsize_narrow_matrix,
    stepsize_widen_matrix,
    stepsize_offset,
    gating_narrow_matrix,
    gating_widen_matrix,
    erasure_lookup_coef,
    lookup_step_fraction,
    diagonal_reward_coef,
    group_layernorm_coef,
):
    highest = lax.Precision.HIGHEST
    segment_length = layer_activation.shape[0]
    stepsize_fraction = query_matrix.shape[1]
    local_attentioners = stepsize_fraction // CHANNELS_PER_ONE
    position = lax.axis_index("seq")
    column = lax.axis_index("tp")
    gathered = lax.all_gather(layer_activation, "tp", axis=1, tiled=True)
    floats = gathered.astype(jnp.float32)
    average = jnp.mean(floats, axis=1, keepdims=True)
    centred = floats - average
    variance = jnp.mean(centred * centred, axis=1, keepdims=True)
    normed = (centred * lax.rsqrt(variance + EPS) * entry_layernorm_coef).astype(jnp.bfloat16)
    normal_f = normed.astype(jnp.float32)
    arrived = from_behind(normed[-1:], "seq", 1)
    bounds = jnp.cumsum(sequence_extents)
    first_token = position * segment_length
    before = first_token - 1
    segment_before = (before >= bounds[0]).astype(jnp.int32) + (before >= bounds[1]).astype(
        jnp.int32
    )
    joined = (segment_before == sequence_label[0]) & (position > 0)
    continues = jnp.concatenate([joined[None], sequence_label[1:] == sequence_label[:-1]])
    previous = jnp.concatenate([arrived.astype(jnp.float32), normal_f[:-1]], axis=0)
    previous = jnp.where(continues[:, None], previous, jnp.zeros_like(previous))
    difference = previous - normal_f

    def blended(which):
        return (normal_f + difference * lagged_blend_coefs[which]).astype(jnp.bfloat16)

    receptance = matmul(blended(0), query_matrix)
    keys = matmul(blended(2), lookup_matrix)
    values = matmul(blended(3), content_matrix)
    decay_hidden = jnp.tanh(matmul(blended(1), forgetting_narrow_matrix)).astype(jnp.bfloat16)
    learn_hidden = matmul(blended(4), stepsize_narrow_matrix).astype(jnp.bfloat16)
    gate_hidden = jax.nn.sigmoid(matmul(blended(5), gating_narrow_matrix)).astype(jnp.bfloat16)
    log_rate = (
        -jax.nn.softplus(-(forgetting_offset + matmul(decay_hidden, forgetting_widen_matrix))) - 0.5
    )
    log_decay = -jnp.exp(log_rate)
    learning = jax.nn.sigmoid(stepsize_offset + matmul(learn_hidden, stepsize_widen_matrix))
    gating_signal = matmul(gate_hidden, gating_widen_matrix)
    removal = (keys * erasure_lookup_coef).reshape(
        segment_length, local_attentioners, CHANNELS_PER_ONE
    )
    removal = removal * lax.rsqrt(jnp.sum(removal * removal, axis=-1, keepdims=True) + 1e-06)
    written = keys * (1.0 + (learning - 1.0) * lookup_step_fraction)
    split_queries = receptance.reshape(segment_length, local_attentioners, CHANNELS_PER_ONE)
    split_lookups = written.reshape(segment_length, local_attentioners, CHANNELS_PER_ONE)
    split_contents = values.reshape(segment_length, local_attentioners, CHANNELS_PER_ONE)
    head_w = log_decay.reshape(segment_length, local_attentioners, CHANNELS_PER_ONE)
    head_a = learning.reshape(segment_length, local_attentioners, CHANNELS_PER_ONE)
    padded_v = jnp.concatenate([split_contents, jnp.zeros_like(split_contents)], axis=-1)
    local_ends = bounds - 1 - first_token
    block_len = min(64, segment_length)
    blocks = segment_length // block_len
    steps_in = jnp.arange(block_len, dtype=jnp.int32)
    strict_lower = steps_in[:, None] > steps_in[None, :]
    with_diag = steps_in[:, None] >= steps_in[None, :]
    unit_eye = jnp.eye(block_len, dtype=jnp.float32)

    def regroup(array):
        return array.reshape((blocks, block_len) + array.shape[1:])

    def block_step(carry, inputs):
        stacked, saved = carry
        block_start, still, r_blk, k_blk, v_blk, n_blk, lw_blk, a_blk = inputs
        restarts = jnp.logical_not(still).astype(jnp.int32)
        epochs = jnp.cumsum(restarts)
        from_start = (epochs == 0).astype(jnp.float32)
        log_total = jnp.cumsum(lw_blk, axis=0)
        query_a = -n_blk * jnp.exp(log_total - lw_blk)
        scaled_beta = n_blk * a_blk * jnp.exp(-log_total)
        scaled_key = k_blk * jnp.exp(-log_total)
        scaled_query = r_blk * jnp.exp(log_total)
        same_run = epochs[:, None] == epochs[None, :]
        strict_mask = (strict_lower & same_run).astype(jnp.float32)
        diag_mask = (with_diag & same_run).astype(jnp.float32)

        def paired(left, right, mask):
            return jnp.einsum("thj,shj->hts", left, right, precision=highest) * mask[None]

        mix_beta = paired(query_a, scaled_beta, strict_mask)
        mix_key = paired(query_a, scaled_key, strict_mask)
        read_beta = paired(scaled_query, scaled_beta, diag_mask)
        read_key = paired(scaled_query, scaled_key, diag_mask)
        from_state = jnp.einsum(
            "thj,hij->hti", query_a * from_start[:, None, None], stacked, precision=highest
        )
        right_side = from_state + jnp.einsum("hts,shi->hti", mix_key, v_blk, precision=highest)
        pseudo = jax.scipy.linalg.solve_triangular(
            unit_eye[None] - mix_beta, right_side, lower=True, unit_diagonal=True
        )
        outputs_blk = jnp.einsum(
            "thj,hij->thi", scaled_query * from_start[:, None, None], stacked, precision=highest
        )
        outputs_blk = outputs_blk + jnp.einsum("hts,hsi->thi", read_beta, pseudo, precision=highest)
        outputs_blk = outputs_blk + jnp.einsum("hts,shi->thi", read_key, v_blk, precision=highest)

        def state_at(moment):
            growth = jnp.exp(lax.dynamic_index_in_dim(log_total, moment, 0, keepdims=False))
            epoch_now = lax.dynamic_index_in_dim(epochs, moment, 0, keepdims=False)
            chosen = ((steps_in <= moment) & (epochs == epoch_now)).astype(jnp.float32)
            weight_beta = scaled_beta * chosen[:, None, None] * growth[None]
            weight_key = scaled_key * chosen[:, None, None] * growth[None]
            start_part = stacked * (growth * (epoch_now == 0).astype(jnp.float32))[:, None, :]
            result = start_part + jnp.einsum("hsi,shj->hij", pseudo, weight_beta, precision=highest)
            return result + jnp.einsum("shi,shj->hij", v_blk, weight_key, precision=highest)

        new_stacked = state_at(jnp.int32(block_len - 1))
        updated = []
        for prompt in range(PROMPTS):
            offset_end = local_ends[prompt] - block_start
            inside = (offset_end >= 0) & (offset_end < block_len)
            moment = jnp.clip(offset_end, 0, block_len - 1)
            updated.append(jnp.where(inside, state_at(moment), saved[prompt]))
        return ((new_stacked, jnp.stack(updated)), outputs_blk)

    identity = jnp.broadcast_to(
        jnp.eye(CHANNELS_PER_ONE, dtype=jnp.float32),
        (local_attentioners, CHANNELS_PER_ONE, CHANNELS_PER_ONE),
    )
    start_stack = jnp.concatenate([jnp.zeros_like(identity), identity], axis=1)
    start_saved = jnp.zeros(
        (PROMPTS, local_attentioners, 2 * CHANNELS_PER_ONE, CHANNELS_PER_ONE), jnp.float32
    )
    block_starts = jnp.arange(blocks, dtype=jnp.int32) * block_len
    scan_inputs = (
        block_starts,
        regroup(continues),
        regroup(split_queries),
        regroup(split_lookups),
        regroup(padded_v),
        regroup(removal),
        regroup(head_w),
        regroup(head_a),
    )
    (final_stack, saved), grouped_out = lax.scan(
        block_step, (start_stack, start_saved), scan_inputs
    )
    outputs = grouped_out.reshape(segment_length, local_attentioners, 2 * CHANNELS_PER_ONE)
    local_state = final_stack[:, :CHANNELS_PER_ONE]
    transition = final_stack[:, CHANNELS_PER_ONE:]

    def passing(turn, incoming):
        return from_behind(
            (compose(incoming, transition) + local_state).astype(jnp.bfloat16), "seq", 1
        ).astype(jnp.float32)

    state_in = lax.fori_loop(0, lax.axis_size("seq") - 1, passing, jnp.zeros_like(local_state))
    readout = outputs[:, :, :CHANNELS_PER_ONE] + jnp.einsum(
        "hij,thj->thi", state_in, outputs[:, :, CHANNELS_PER_ONE:], precision=highest
    )
    centre = readout - jnp.mean(readout, axis=-1, keepdims=True)
    spread = jnp.mean(centre * centre, axis=-1, keepdims=True)
    group_standardized = (
        centre
        * lax.rsqrt(spread + GROUP_EPS)
        * group_layernorm_coef.reshape(local_attentioners, CHANNELS_PER_ONE)
    )
    diagonal_reward = (
        jnp.sum(
            split_queries
            * split_lookups
            * diagonal_reward_coef.reshape(local_attentioners, CHANNELS_PER_ONE),
            axis=-1,
            keepdims=True,
        )
        * split_contents
    )
    visible_entries = (
        (group_standardized + diagonal_reward).reshape(segment_length, stepsize_fraction)
        * gating_signal
    ).astype(jnp.bfloat16)
    partial_value = matmul(visible_entries, readout_matrix)
    summed = lax.psum_scatter(
        partial_value.astype(jnp.bfloat16), "tp", scatter_dimension=1, tiled=True
    ).astype(jnp.float32)
    mixed = (summed + layer_activation.astype(jnp.float32)).astype(jnp.bfloat16)
    final_states = jnp.zeros(
        (1, local_attentioners, CHANNELS_PER_ONE, CHANNELS_PER_ONE), jnp.float32
    )
    final_rows = jnp.zeros((1, stepsize_fraction), jnp.bfloat16)
    for prompt in range(PROMPTS):
        last_token = bounds[prompt] - 1
        holder = last_token // segment_length
        inside = jnp.clip(last_token - first_token, 0, segment_length - 1)
        recorded = saved[prompt]
        state_end = (
            compose(state_in, recorded[:, CHANNELS_PER_ONE:]) + recorded[:, :CHANNELS_PER_ONE]
        )
        row_end = lax.dynamic_slice(
            normal_f, (inside, column * stepsize_fraction), (1, stepsize_fraction)
        )
        got_state, got_row = (
            broadcast(state_end.astype(jnp.bfloat16), "seq", holder).astype(state_end.dtype),
            broadcast(row_end.astype(jnp.bfloat16), "seq", holder).astype(row_end.dtype),
        )
        is_owner = position == destination_slots[prompt]
        final_states = jnp.where(is_owner, got_state[None], final_states)
        final_rows = jnp.where(is_owner, got_row.astype(jnp.bfloat16), final_rows)
    return (mixed, final_states, final_rows)


def solution(mesh):
    return jax.shard_map(
        on_device,
        mesh=mesh,
        in_specs=(
            P("seq", "tp"),
            P("seq"),
            P(),
            P(),
            P(),
            P(),
            P(None, "tp"),
            P(None, "tp"),
            P(None, "tp"),
            P("tp", None),
            P(),
            P(None, "tp"),
            P("tp"),
            P(),
            P(None, "tp"),
            P("tp"),
            P(),
            P(None, "tp"),
            P("tp"),
            P("tp"),
            P("tp"),
            P("tp"),
        ),
        out_specs=(P("seq", "tp"), P("seq", "tp", None, None), P("seq", "tp")),
        check_vma=False,
    )
```

profile of v0, /device:TPU:0, one launch (start us, length us, event | category | flops | bytes accessed | tf_op | source)
XLA Modules:
  0.0 698.0 jit_solution(5239069506846674704)
XLA Ops:
  14.6 17.4 %all-gather.2.cloned.1.call-done = bf16[384,2048]{1,0:T(8,128)(2,1)} async-done(((bf16[384,512]{1,0:T(8,128)(2,1)}), bf16[384,2048]{1,0:T(8,128)(2,1)}) %all-gather.2.cloned.1.call-update) | async-done | bytes 1572880 | tf_op jit(solution)/shard_map/all_gather | solution.py:61
  51.7 5.1 fusion.72
  59.3 5.5 fusion.149
  68.7 5.1 fusion.139
  80.6 4.5 fusion.74
  92.1 414.9 %while.27 = (s32[]{:T(128)}, f32[8,128,64]{1,2,0:T(8,128)S(1)}, f32[2,8,128,64]{2,3,1,0:T(8,128)}, f32[6,64,8,128]{3,2,1,0:T(8,128)}, f32[6,64,8,64]{3,2,1,0:T(8...) while((s32[]{:T(128)}, f32[8,128,64]{1,2,0:T(8,128)S(1)}, ...), condition=%wide.region_7.8_spmd.clone.clone, body=%wide.region_4.7_spmd.clone.clone.sunk | while | flops 708762112 | bytes 20262212 | solution.py:191
  108.9 40.7 %custom-call.9 = f32[8,1,64,64]{2,3,1,0:T(8,128)} custom-call(f32[8,1,64,64]{3,2,1,0:T(8,128)} %fusion.259), custom_call_target="InvertDiagBlocksLowerTriangular" | custom-call | tf_op jit(solution)/shard_map/while/body/eval_jaxpr/jit(_solve_triangular)/vmap()/triangular_solve | solution.py:144
  178.1 40.7 %custom-call.9 = f32[8,1,64,64]{2,3,1,0:T(8,128)} custom-call(f32[8,1,64,64]{3,2,1,0:T(8,128)} %fusion.259), custom_call_target="InvertDiagBlocksLowerTriangular" | custom-call | tf_op jit(solution)/shard_map/while/body/eval_jaxpr/jit(_solve_triangular)/vmap()/triangular_solve | solution.py:144
  247.2 40.7 %custom-call.9 = f32[8,1,64,64]{2,3,1,0:T(8,128)} custom-call(f32[8,1,64,64]{3,2,1,0:T(8,128)} %fusion.259), custom_call_target="InvertDiagBlocksLowerTriangular" | custom-call | tf_op jit(solution)/shard_map/while/body/eval_jaxpr/jit(_solve_triangular)/vmap()/triangular_solve | solution.py:144
  316.4 40.7 %custom-call.9 = f32[8,1,64,64]{2,3,1,0:T(8,128)} custom-call(f32[8,1,64,64]{3,2,1,0:T(8,128)} %fusion.259), custom_call_target="InvertDiagBlocksLowerTriangular" | custom-call | tf_op jit(solution)/shard_map/while/body/eval_jaxpr/jit(_solve_triangular)/vmap()/triangular_solve | solution.py:144
  385.5 40.7 %custom-call.9 = f32[8,1,64,64]{2,3,1,0:T(8,128)} custom-call(f32[8,1,64,64]{3,2,1,0:T(8,128)} %fusion.259), custom_call_target="InvertDiagBlocksLowerTriangular" | custom-call | tf_op jit(solution)/shard_map/while/body/eval_jaxpr/jit(_solve_triangular)/vmap()/triangular_solve | solution.py:144
  454.7 40.7 %custom-call.9 = f32[8,1,64,64]{2,3,1,0:T(8,128)} custom-call(f32[8,1,64,64]{3,2,1,0:T(8,128)} %fusion.259), custom_call_target="InvertDiagBlocksLowerTriangular" | custom-call | tf_op jit(solution)/shard_map/while/body/eval_jaxpr/jit(_solve_triangular)/vmap()/triangular_solve | solution.py:144
  517.1 55.1 %while.28 = (s32[]{:T(128)}, f32[8,64,64]{2,1,0:T(8,128)S(1)}, f32[8,64,64]{2,1,0:T(8,128)S(1)}, f32[8,64,64]{2,1,0:T(8,128)S(1)}, s32[]{:T(128)}, /*index=5*/s32[]{:T(128)}) while((s32[]{:T(128)}, f32[8,64,64]{2,1,0:T(8,128)S(1)}, f32[8,64,64]{2,1,0:T(8,128)S(1)}, f32[8,64,64]{2,1,0:T(8,128)S(1)}, s32[]{:T(128)}, ...), condition=%wide.region_9.10_spmd.clone, body=%wide.region_8.9_spmd.clone.sunk | while | flops 25296900 | bytes 917623 | solution.py:203
  524.1 4.4 collective-permute-start
  531.4 4.4 collective-permute-start
  538.7 5.2 collective-permute-start
  546.9 5.3 collective-permute-start
  555.1 5.3 collective-permute-start
  563.8 5.6 collective-permute-start
  572.1 4.1 fusion.157
  579.0 4.4 fusion.116
  592.5 22.7 %all-reduce.2 = (bf16[1,512]{1,0:T(2,128)(2,1)S(1)}, bf16[1,512]{1,0:T(2,128)(2,1)S(1)}) all-reduce(bf16[1,512]{1,0:T(2,128)(2,1)S(1)} %get-tuple-element.333, bf16[1,512]{1,0:T(2,128)(2,1)S(1)} %get-tuple-element.332), channel_id=1, replica_groups=mesh['seq'=8,'tp'=4] {'seq'}, use_global_device_ids=true, to_apply=%region_16.17 | all-reduce | flops 1024 | bytes 4096 | tf_op jit(solution)/shard_map/psum | solution.py:20
  615.9 43.6 %all-reduce.6.cloned.1.call-done = (bf16[8,64,64]{2,1,0:T(8,128)(2,1)}, bf16[8,64,64]{2,1,0:T(8,128)(2,1)}) async-done(((bf16[8,64,64]{2,1,0:T(8,128)(2,1)}, bf16[8,64,64]{2,1,0:T(8,128)(2,1)}), (bf16[8,64,64]{2,1,0:T(8,128)(2,1)}, bf16[8,64,64]{2,1,0:T(8,128)(2,1)})) %all-reduce.6.cloned.1.call-update) | async-done | bytes 131088 | tf_op jit(solution)/shard_map/psum | solution.py:20
  661.1 28.5 %reduce-scatter.2.cloned.1.call-done = bf16[384,512]{1,0:T(8,128)(2,1)} async-done(((bf16[384,2048]{1,0:T(8,128)(2,1)}), bf16[384,512]{1,0:T(8,128)(2,1)}) %reduce-scatter.2.cloned.1.call-update) | async-done | bytes 393232 | tf_op jit(solution)/shard_map/reduce_scatter | solution.py:229
  (360 shorter events, 234.6 us)
Async XLA Ops:
  7.2 52.1 %copy-start = (bf16[2048,512]{1,0:T(8,128)(2,1)S(1)}, bf16[2048,512]{1,0:T(8,128)(2,1)}, u32[]{:S(2)}) copy-start(bf16[2048,512]{1,0:T(8,128)(2,1)} %param.33) | copy-start | bytes 6291460
  7.2 28.6 %copy-start.15 = (f32[2048]{0:T(1024)S(1)}, f32[2048]{0:T(1024)}, u32[]{:S(2)}) copy-start(f32[2048]{0:T(1024)} %param.30) | copy-start | bytes 24580
  7.2 24.8 %all-gather.2.cloned.1.call-start = ((), (), s32[]{:S(2)}) async-start(), calls=%async_computation.1 | async-start | bytes 1966080 | tf_op jit(solution)/shard_map/all_gather | solution.py:61
  7.9 651.5 %all-reduce.6.cloned.1.call-start = ((), (), s32[]{:S(2)}) async-start(), calls=%async_computation.3 | async-start | bytes 524288 | tf_op jit(solution)/shard_map/psum | solution.py:20
  14.6 27.9 %copy-start.16 = (f32[512]{0:T(512)S(1)}, f32[512]{0:T(512)}, u32[]{:S(2)}) copy-start(f32[512]{0:T(512)} %param.46) | copy-start | bytes 6148
  14.6 28.0 %copy-start.17 = (f32[512]{0:T(512)S(1)}, f32[512]{0:T(512)}, u32[]{:S(2)}) copy-start(f32[512]{0:T(512)} %param.47) | copy-start | bytes 6148
  37.5 8.7 %collective-permute-start.1 = (bf16[1,2048]{1,0:T(2,128)(2,1)S(1)}, bf16[1,2048]{1,0:T(2,128)(2,1)S(1)}, u32[]{:S(2)}, u32[]{:S(2)}) collective-permute-start(bf16[1,2048]{1,0:T(2,128)(2,1)S(1)} %slice.132), channel_id=1, source_target_pairs={{0,4},{4,8},{8,12},{12,16},{16,20},{20,24},{24,28},{1,5},{5,9},{9,... | collective-permute-start | bytes 12296 | tf_op jit(solution)/shard_map/ppermute | solution.py:15
  51.7 7.6 %copy-start.21 = (f32[512]{0:T(512)S(1)}, f32[512]{0:T(512)}, u32[]{:S(2)}) copy-start(f32[512]{0:T(512)} %param.44) | copy-start | bytes 6148
  51.7 7.6 %copy-start.22 = (f32[512]{0:T(512)S(1)}, f32[512]{0:T(512)}, u32[]{:S(2)}) copy-start(f32[512]{0:T(512)} %param.45) | copy-start | bytes 6148
  73.8 5.3 copy-start.14
  85.1 6.1 copy-start.9
  149.6 4.9 copy-start.1
  495.4 4.9 copy-start.1
  512.1 4.9 copy-start.3
  517.4 6.2 collective-permute-start
  524.1 6.9 collective-permute-start
  531.4 6.9 collective-permute-start
  538.7 7.7 %collective-permute-start = (bf16[8,64,64]{2,1,0:T(8,128)(2,1)S(1)}, bf16[8,64,64]{2,1,0:T(8,128)(2,1)S(1)}, u32[]{:S(2)}, u32[]{:S(2)}) collective-permute-start(bf16[8,64,64]{2,1,0:T(8,128)(2,1)S(1)} %fusion.267), channel_id=1, source_target_pairs={{0,4},{4,8},{8,12},{12,16},{16,20},{20,24},{24,28},{1,5},{5,9},{9,... | collective-permute-start | bytes 196616 | tf_op jit(solution)/shard_map/while/body/eval_jaxpr/ppermute | solution.py:15
  546.9 7.8 %collective-permute-start = (bf16[8,64,64]{2,1,0:T(8,128)(2,1)S(1)}, bf16[8,64,64]{2,1,0:T(8,128)(2,1)S(1)}, u32[]{:S(2)}, u32[]{:S(2)}) collective-permute-start(bf16[8,64,64]{2,1,0:T(8,128)(2,1)S(1)} %fusion.267), channel_id=1, source_target_pairs={{0,4},{4,8},{8,12},{12,16},{16,20},{20,24},{24,28},{1,5},{5,9},{9,... | collective-permute-start | bytes 196616 | tf_op jit(solution)/shard_map/while/body/eval_jaxpr/ppermute | solution.py:15
  555.1 8.3 %collective-permute-start = (bf16[8,64,64]{2,1,0:T(8,128)(2,1)S(1)}, bf16[8,64,64]{2,1,0:T(8,128)(2,1)S(1)}, u32[]{:S(2)}, u32[]{:S(2)}) collective-permute-start(bf16[8,64,64]{2,1,0:T(8,128)(2,1)S(1)} %fusion.267), channel_id=1, source_target_pairs={{0,4},{4,8},{8,12},{12,16},{16,20},{20,24},{24,28},{1,5},{5,9},{9,... | collective-permute-start | bytes 196616 | tf_op jit(solution)/shard_map/while/body/eval_jaxpr/ppermute | solution.py:15
  563.8 8.1 %collective-permute-start = (bf16[8,64,64]{2,1,0:T(8,128)(2,1)S(1)}, bf16[8,64,64]{2,1,0:T(8,128)(2,1)S(1)}, u32[]{:S(2)}, u32[]{:S(2)}) collective-permute-start(bf16[8,64,64]{2,1,0:T(8,128)(2,1)S(1)} %fusion.267), channel_id=1, source_target_pairs={{0,4},{4,8},{8,12},{12,16},{16,20},{20,24},{24,28},{1,5},{5,9},{9,... | collective-permute-start | bytes 196616 | tf_op jit(solution)/shard_map/while/body/eval_jaxpr/ppermute | solution.py:15
  579.0 5.5 copy-start.12
  585.6 104.1 %copy-start.11 = (bf16[384,512]{1,0:T(8,128)(2,1)S(1)}, bf16[384,512]{1,0:T(8,128)(2,1)}, u32[]{:S(2)}) copy-start(bf16[384,512]{1,0:T(8,128)(2,1)} %param.26) | copy-start | bytes 1179652
  585.6 104.0 %reduce-scatter.2.cloned.1.call-start = ((), (), s32[]{:S(2)}) async-start(), calls=%async_computation.2 | async-start | bytes 1966080 | tf_op jit(solution)/shard_map/reduce_scatter | solution.py:229
  (21 other events, 74.8 us)
Sparse Core Ops, SparseCore 0:
  9.6 22.3 all-gather.1
  585.7 73.6 all-reduce.5
  662.1 27.4 reduce-scatter.1
where the time goes:
time: 701 us; the launch traced here: 698 us
  other arithmetic  299 us (43%)
  matrix products  120 us (17%)
  waiting for transfers between devices  109 us (16%)
  local copies, waits for them, and re-layouts  62.6 us (9%)
  starting transfers between devices  36.9 us (5%)
  loops' own time  29.5 us (4%)
  blocking collectives  22.7 us (3%)
  between operations  18.8 us (3%)
    another operation x18, other arithmetic, block_step(): jax.scipy.linalg.solve_triangular(unit_eye[None] - mix_beta, right_side,...  245 us
    psum x1, waiting for transfers between devices, broadcast(): return lax.psum(kept, axis)  43.6 us
    ppermute x8, starting transfers between devices, from_behind(): return lax.ppermute(array, axis, pairs)  36.8 us
    dot_general x7, matrix products, matmul(): return jnp.dot(left, right, preferred_element_type=jnp.float32)  32.6 us
    another operation x1, loops' own time, on_device(): lax.scan(block_step, (start_stack, start_saved), scan_inputs)  29.1 us
    reduce_scatter x1, waiting for transfers between devices, on_device(): lax.psum_scatter(partial_value.astype(jnp.bfloat16), 'tp', scatter_dimens...  28.5 us
    psum x1, blocking collectives, broadcast(): return lax.psum(kept, axis)  22.7 us
    dot_general x24, matrix products, paired(): jnp.einsum('thj,shj->hts', left, right, precision=highest) * mask[None]  18.6 us
  transfers between devices with their start and end apart: 11, of which 10 were waited for; matrix products, arithmetic and copies ran while one was open for 2% of the time, Pallas kernels for 0%

commit v1 on v0

--- a/solution.py
+++ b/solution.py
@@ -7,6 +7,27 @@
 PROMPTS = 2
 EPS = 1e-05
 GROUP_EPS = 0.00064
+
+
+def ring_gather(array, axis, dim):
+    size, index, extent = (lax.axis_size(axis), lax.axis_index(axis), array.shape[dim])
+    ahead = [(i, (i + 1) % size) for i in range(size)]
+    backward = [(i, (i - 1) % size) for i in range(size)]
+    out = jnp.zeros((*array.shape[:dim], size * extent, *array.shape[dim + 1 :]), array.dtype)
+    out = lax.dynamic_update_slice_in_dim(out, array, index * extent, axis=dim)
+    from_left = from_right = array
+    halfway = size // 2
+    for lap in range(1, halfway + 1):
+        from_left = lax.ppermute(from_left, axis, ahead)
+        out = lax.dynamic_update_slice_in_dim(
+            out, from_left, (index - lap) % size * extent, axis=dim
+        )
+        if lap < size - halfway:
+            from_right = lax.ppermute(from_right, axis, backward)
+            out = lax.dynamic_update_slice_in_dim(
+                out, from_right, (index + lap) % size * extent, axis=dim
+            )
+    return out
 
 
 def from_behind(array, axis, by):
@@ -58,7 +79,7 @@
     local_attentioners = stepsize_fraction // CHANNELS_PER_ONE
     position = lax.axis_index("seq")
     column = lax.axis_index("tp")
-    gathered = lax.all_gather(layer_activation, "tp", axis=1, tiled=True)
+    gathered = ring_gather(layer_activation, "tp", 1)
     floats = gathered.astype(jnp.float32)
     average = jnp.mean(floats, axis=1, keepdims=True)
     centred = floats - average

time: 701 us -> 669 us (0.954)
  waiting for transfers between devices: 109 us -> 69.2 us
    reduce_scatter x1, waiting for transfers between devices: 28.5 us -> 0.01 us  [on_device(): lax.psum_scatter(partial_value.astype(jnp.bfloat16), 'tp', scatter_dimens...]
    all_gather x1 -> x0, waiting for transfers between devices: 17.4 us -> none  [on_device(): gathered = lax.all_gather(layer_activation, 'tp', axis=1, tiled=True)]
  transfers between devices with their start and end apart: 11 -> 13, of which waited for: 10 -> 10; matrix products, arithmetic and copies ran while one was open for 2% -> 2% of each run, Pallas kernels for 0% -> 0%
where the time goes in v1:
time: 669 us; the launch traced here: 666 us
  other arithmetic  296 us (44%)
  matrix products  120 us (18%)
  waiting for transfers between devices  69.2 us (10%)
  local copies, waits for them, and re-layouts  64.5 us (10%)
  starting transfers between devices  43.9 us (7%)
  loops' own time  28.8 us (4%)
  blocking collectives  23 us (3%)
  between operations  20.6 us (3%)
    another operation x18, other arithmetic, block_step(): jax.scipy.linalg.solve_triangular(unit_eye[None] - mix_beta, right_side,...  245 us
    psum x1, waiting for transfers between devices, broadcast(): return lax.psum(kept, axis)  45.8 us
    ppermute x8, starting transfers between devices, from_behind(): return lax.ppermute(array, axis, pairs)  38.8 us
    dot_general x7, matrix products, matmul(): return jnp.dot(left, right, preferred_element_type=jnp.float32)  32.5 us
    another operation x1, loops' own time, on_device(): lax.scan(block_step, (start_stack, start_saved), scan_inputs)  28.3 us
    psum x1, blocking collectives, broadcast(): return lax.psum(kept, axis)  23 us
    dot_general x24, matrix products, paired(): jnp.einsum('thj,shj->hts', left, right, precision=highest) * mask[None]  18.6 us
    ppermute x8, waiting for transfers between devices, from_behind(): return lax.ppermute(array, axis, pairs)  18.4 us
  transfers between devices with their start and end apart: 13, of which 10 were waited for; matrix products, arithmetic and copies ran while one was open for 2% of the time, Pallas kernels for 0%

profile of v1, /device:TPU:0, one launch (start us, length us, event | category | flops | bytes accessed | tf_op | source)
XLA Modules:
  0.0 665.9 jit_solution(1374590591658182451)
XLA Ops:
  28.7 5.2 collective-permute-start.4
  44.7 5.0 fusion.72
  52.3 5.5 fusion.149
  61.7 5.1 fusion.139
  73.6 4.5 fusion.74
  85.1 413.9 %while.27 = (s32[]{:T(128)}, f32[8,128,64]{1,2,0:T(8,128)S(1)}, f32[2,8,128,64]{2,3,1,0:T(8,128)}, f32[6,64,8,128]{3,2,1,0:T(8,128)}, f32[6,64,8,64]{3,2,1,0:T(8...) while((s32[]{:T(128)}, f32[8,128,64]{1,2,0:T(8,128)S(1)}, ...), condition=%wide.region_7.8_spmd.clone.clone, body=%wide.region_4.7_spmd.clone.clone.sunk | while | flops 708762112 | bytes 20262212 | solution.py:212
  101.8 40.7 %custom-call.9 = f32[8,1,64,64]{2,3,1,0:T(8,128)} custom-call(f32[8,1,64,64]{3,2,1,0:T(8,128)} %fusion.259), custom_call_target="InvertDiagBlocksLowerTriangular" | custom-call | tf_op jit(solution)/shard_map/while/body/eval_jaxpr/jit(_solve_triangular)/vmap()/triangular_solve | solution.py:165
  170.7 40.7 %custom-call.9 = f32[8,1,64,64]{2,3,1,0:T(8,128)} custom-call(f32[8,1,64,64]{3,2,1,0:T(8,128)} %fusion.259), custom_call_target="InvertDiagBlocksLowerTriangular" | custom-call | tf_op jit(solution)/shard_map/while/body/eval_jaxpr/jit(_solve_triangular)/vmap()/triangular_solve | solution.py:165
  239.7 40.7 %custom-call.9 = f32[8,1,64,64]{2,3,1,0:T(8,128)} custom-call(f32[8,1,64,64]{3,2,1,0:T(8,128)} %fusion.259), custom_call_target="InvertDiagBlocksLowerTriangular" | custom-call | tf_op jit(solution)/shard_map/while/body/eval_jaxpr/jit(_solve_triangular)/vmap()/triangular_solve | solution.py:165
  308.7 40.7 %custom-call.9 = f32[8,1,64,64]{2,3,1,0:T(8,128)} custom-call(f32[8,1,64,64]{3,2,1,0:T(8,128)} %fusion.259), custom_call_target="InvertDiagBlocksLowerTriangular" | custom-call | tf_op jit(solution)/shard_map/while/body/eval_jaxpr/jit(_solve_triangular)/vmap()/triangular_solve | solution.py:165
  377.7 40.7 %custom-call.9 = f32[8,1,64,64]{2,3,1,0:T(8,128)} custom-call(f32[8,1,64,64]{3,2,1,0:T(8,128)} %fusion.259), custom_call_target="InvertDiagBlocksLowerTriangular" | custom-call | tf_op jit(solution)/shard_map/while/body/eval_jaxpr/jit(_solve_triangular)/vmap()/triangular_solve | solution.py:165
  446.7 40.7 %custom-call.9 = f32[8,1,64,64]{2,3,1,0:T(8,128)} custom-call(f32[8,1,64,64]{3,2,1,0:T(8,128)} %fusion.259), custom_call_target="InvertDiagBlocksLowerTriangular" | custom-call | tf_op jit(solution)/shard_map/while/body/eval_jaxpr/jit(_solve_triangular)/vmap()/triangular_solve | solution.py:165
  509.8 55.3 %while.28 = (s32[]{:T(128)}, f32[8,64,64]{2,1,0:T(8,128)S(1)}, f32[8,64,64]{2,1,0:T(8,128)S(1)}, f32[8,64,64]{2,1,0:T(8,128)S(1)}, s32[]{:T(128)}, /*index=5*/s32[]{:T(128)}) while((s32[]{:T(128)}, f32[8,64,64]{2,1,0:T(8,128)S(1)}, f32[8,64,64]{2,1,0:T(8,128)S(1)}, f32[8,64,64]{2,1,0:T(8,128)S(1)}, s32[]{:T(128)}, ...), condition=%wide.region_9.10_spmd.clone, body=%wide.region_8.9_spmd.clone.sunk | while | flops 25296900 | bytes 917623 | solution.py:224
  516.8 4.4 collective-permute-start
  524.1 4.4 collective-permute-start
  531.4 5.2 collective-permute-start
  539.6 5.3 collective-permute-start
  547.8 5.3 collective-permute-start
  556.7 5.6 collective-permute-start
  565.1 4.1 fusion.157
  572.0 4.4 fusion.116
  578.6 4.0 convolution_convert_fusion
  585.4 23.0 %all-reduce.2 = (bf16[1,512]{1,0:T(2,128)(2,1)S(1)}, bf16[1,512]{1,0:T(2,128)(2,1)S(1)}) all-reduce(bf16[1,512]{1,0:T(2,128)(2,1)S(1)} %get-tuple-element.333, bf16[1,512]{1,0:T(2,128)(2,1)S(1)} %get-tuple-element.332), channel_id=1, replica_groups=mesh['seq'=8,'tp'=4] {'seq'}, use_global_device_ids=true, to_apply=%region_16.17 | all-reduce | flops 1024 | bytes 4096 | tf_op jit(solution)/shard_map/psum | solution.py:41
  609.0 45.8 %all-reduce.6.cloned.1.call-done = (bf16[8,64,64]{2,1,0:T(8,128)(2,1)}, bf16[8,64,64]{2,1,0:T(8,128)(2,1)}) async-done(((bf16[8,64,64]{2,1,0:T(8,128)(2,1)}, bf16[8,64,64]{2,1,0:T(8,128)(2,1)}), (bf16[8,64,64]{2,1,0:T(8,128)(2,1)}, bf16[8,64,64]{2,1,0:T(8,128)(2,1)})) %all-reduce.6.cloned.1.call-update) | async-done | bytes 131088 | tf_op jit(solution)/shard_map/psum | solution.py:41
  (372 shorter events, 235.5 us)
Async XLA Ops:
  8.0 44.3 %copy-start = (bf16[2048,512]{1,0:T(8,128)(2,1)S(1)}, bf16[2048,512]{1,0:T(8,128)(2,1)}, u32[]{:S(2)}) copy-start(bf16[2048,512]{1,0:T(8,128)(2,1)} %param.33) | copy-start | bytes 6291460
  8.0 15.7 %copy-start.11 = (bf16[384,512]{1,0:T(8,128)(2,1)S(1)}, bf16[384,512]{1,0:T(8,128)(2,1)}, u32[]{:S(2)}) copy-start(bf16[384,512]{1,0:T(8,128)(2,1)} %param.26) | copy-start | bytes 1179652
  8.0 646.8 %all-reduce.6.cloned.1.call-start = ((), (), s32[]{:S(2)}) async-start(), calls=%async_computation.2 | async-start | bytes 524288 | tf_op jit(solution)/shard_map/psum | solution.py:41
  8.1 9.7 %collective-permute-start.1 = (bf16[384,512]{1,0:T(8,128)(2,1)}, bf16[384,512]{1,0:T(8,128)(2,1)S(1)}, u32[]{:S(2)}, u32[]{:S(2)}) collective-permute-start(bf16[384,512]{1,0:T(8,128)(2,1)} %param.26), channel_id=1, source_target_pairs={{0,1},{1,2},{2,3},{3,0},{4,5},{5,6},{6,7},{7,4},{8,9},{9,10},{10,1... | collective-permute-start | bytes 1179656 | tf_op jit(solution)/shard_map/ppermute | solution.py:21
  8.6 15.2 %collective-permute-start.2 = (bf16[384,512]{1,0:T(8,128)(2,1)}, bf16[384,512]{1,0:T(8,128)(2,1)S(1)}, u32[]{:S(2)}, u32[]{:S(2)}) collective-permute-start(bf16[384,512]{1,0:T(8,128)(2,1)} %param.26), channel_id=1, source_target_pairs={{0,3},{1,0},{2,1},{3,2},{4,7},{5,4},{6,5},{7,6},{8,11},{9,8},{10,9... | collective-permute-start | bytes 1179656 | tf_op jit(solution)/shard_map/ppermute | solution.py:26
  17.7 7.3 %collective-permute-start.3 = (bf16[384,512]{1,0:T(8,128)(2,1)S(1)}, bf16[384,512]{1,0:T(8,128)(2,1)}, u32[]{:S(2)}, u32[]{:S(2)}) collective-permute-start(bf16[384,512]{1,0:T(8,128)(2,1)S(1)} %collective-permute-done.1), channel_id=1, source_target_pairs={{0,1},{1,2},{2,3},{3,0},{4,5},{5,6},{6,7},{7,4},{8,9},{9,10},{10,1... | collective-permute-start | bytes 1179656 | tf_op jit(solution)/shard_map/ppermute | solution.py:21
  26.4 9.1 %copy-start.18 = (f32[512]{0:T(512)S(1)}, f32[512]{0:T(512)}, u32[]{:S(2)}) copy-start(f32[512]{0:T(512)} %param.46) | copy-start | bytes 6148
  26.4 9.2 %copy-start.19 = (f32[512]{0:T(512)S(1)}, f32[512]{0:T(512)}, u32[]{:S(2)}) copy-start(f32[512]{0:T(512)} %param.47) | copy-start | bytes 6148
  28.7 10.6 %collective-permute-start.4 = (bf16[1,2048]{1,0:T(2,128)(2,1)S(1)}, bf16[1,2048]{1,0:T(2,128)(2,1)S(1)}, u32[]{:S(2)}, u32[]{:S(2)}) collective-permute-start(bf16[1,2048]{1,0:T(2,128)(2,1)S(1)} %slice.132), channel_id=1, source_target_pairs={{0,4},{4,8},{8,12},{12,16},{16,20},{20,24},{24,28},{1,5},{5,9},{9,... | collective-permute-start | bytes 12296 | tf_op jit(solution)/shard_map/ppermute | solution.py:36
  66.8 5.3 copy-start.15
  211.4 4.9 copy-start.1
  280.4 4.9 copy-start.1
  349.4 4.9 copy-start.1
  510.2 6.1 collective-permute-start
  516.8 6.9 %collective-permute-start = (bf16[8,64,64]{2,1,0:T(8,128)(2,1)S(1)}, bf16[8,64,64]{2,1,0:T(8,128)(2,1)S(1)}, u32[]{:S(2)}, u32[]{:S(2)}) collective-permute-start(bf16[8,64,64]{2,1,0:T(8,128)(2,1)S(1)} %fusion.267), channel_id=1, source_target_pairs={{0,4},{4,8},{8,12},{12,16},{16,20},{20,24},{24,28},{1,5},{5,9},{9,... | collective-permute-start | bytes 196616 | tf_op jit(solution)/shard_map/while/body/eval_jaxpr/ppermute | solution.py:36
  524.1 6.9 %collective-permute-start = (bf16[8,64,64]{2,1,0:T(8,128)(2,1)S(1)}, bf16[8,64,64]{2,1,0:T(8,128)(2,1)S(1)}, u32[]{:S(2)}, u32[]{:S(2)}) collective-permute-start(bf16[8,64,64]{2,1,0:T(8,128)(2,1)S(1)} %fusion.267), channel_id=1, source_target_pairs={{0,4},{4,8},{8,12},{12,16},{16,20},{20,24},{24,28},{1,5},{5,9},{9,... | collective-permute-start | bytes 196616 | tf_op jit(solution)/shard_map/while/body/eval_jaxpr/ppermute | solution.py:36
  531.4 7.7 %collective-permute-start = (bf16[8,64,64]{2,1,0:T(8,128)(2,1)S(1)}, bf16[8,64,64]{2,1,0:T(8,128)(2,1)S(1)}, u32[]{:S(2)}, u32[]{:S(2)}) collective-permute-start(bf16[8,64,64]{2,1,0:T(8,128)(2,1)S(1)} %fusion.267), channel_id=1, source_target_pairs={{0,4},{4,8},{8,12},{12,16},{16,20},{20,24},{24,28},{1,5},{5,9},{9,... | collective-permute-start | bytes 196616 | tf_op jit(solution)/shard_map/while/body/eval_jaxpr/ppermute | solution.py:36
  539.6 7.8 %collective-permute-start = (bf16[8,64,64]{2,1,0:T(8,128)(2,1)S(1)}, bf16[8,64,64]{2,1,0:T(8,128)(2,1)S(1)}, u32[]{:S(2)}, u32[]{:S(2)}) collective-permute-start(bf16[8,64,64]{2,1,0:T(8,128)(2,1)S(1)} %fusion.267), channel_id=1, source_target_pairs={{0,4},{4,8},{8,12},{12,16},{16,20},{20,24},{24,28},{1,5},{5,9},{9,... | collective-permute-start | bytes 196616 | tf_op jit(solution)/shard_map/while/body/eval_jaxpr/ppermute | solution.py:36
  547.8 8.5 %collective-permute-start = (bf16[8,64,64]{2,1,0:T(8,128)(2,1)S(1)}, bf16[8,64,64]{2,1,0:T(8,128)(2,1)S(1)}, u32[]{:S(2)}, u32[]{:S(2)}) collective-permute-start(bf16[8,64,64]{2,1,0:T(8,128)(2,1)S(1)} %fusion.267), channel_id=1, source_target_pairs={{0,4},{4,8},{8,12},{12,16},{16,20},{20,24},{24,28},{1,5},{5,9},{9,... | collective-permute-start | bytes 196616 | tf_op jit(solution)/shard_map/while/body/eval_jaxpr/ppermute | solution.py:36
  556.7 8.1 %collective-permute-start = (bf16[8,64,64]{2,1,0:T(8,128)(2,1)S(1)}, bf16[8,64,64]{2,1,0:T(8,128)(2,1)S(1)}, u32[]{:S(2)}, u32[]{:S(2)}) collective-permute-start(bf16[8,64,64]{2,1,0:T(8,128)(2,1)S(1)} %fusion.267), channel_id=1, source_target_pairs={{0,4},{4,8},{8,12},{12,16},{16,20},{20,24},{24,28},{1,5},{5,9},{9,... | collective-permute-start | bytes 196616 | tf_op jit(solution)/shard_map/while/body/eval_jaxpr/ppermute | solution.py:36
  572.0 5.5 copy-start.13
  572.0 6.6 copy-start.16
  578.6 78.0 %reduce-scatter.2.cloned.1.call-start = ((), (), s32[]{:S(2)}) async-start(), calls=%async_computation.1 | async-start | bytes 1966080 | tf_op jit(solution)/shard_map/reduce_scatter | solution.py:250
  582.6 73.9 %copy-start.12 = (bf16[384,512]{1,0:T(8,128)(2,1)S(1)}, bf16[384,512]{1,0:T(8,128)(2,1)}, u32[]{:S(2)}) copy-start(bf16[384,512]{1,0:T(8,128)(2,1)} %param.26) | copy-start | bytes 1179652
  (25 other events, 75.3 us)
Sparse Core Ops, SparseCore 0:
  578.7 76.1 all-reduce.5
Sparse Core Ops, SparseCore 1:
  582.7 33.4 reduce-scatter.1
